TPU v7x, 128 devices: a whole 4x4x4 slice. The times are simulated.
128 devices in a mesh: dp: 8 (over x, core), seq: 16 (over y, z).
Axes of the slice: x: 4, y: 4, z: 4, core: 2. Of those that a mesh axis runs over, the one named last changes fastest.
Arguments:
- queries: bfloat16 [16, 98304, 128], P(None, ('dp', 'seq')), parts along dimension 1, may hold values from -6 to 6
- key_rows: bfloat16 [16, 98304, 128], P(None, ('dp', 'seq')), parts along dimension 1, may hold values from -6 to 6
- value_rows: bfloat16 [16, 98304, 128], P(None, ('dp', 'seq')), parts along dimension 1, may hold values from -6 to 6
- out_grad: bfloat16 [16, 98304, 128], P(None, ('dp', 'seq')), parts along dimension 1, may hold values from -6 to 6
Outputs:
- attended: bfloat16 [16, 98304, 128], P(None, ('dp', 'seq')), parts along dimension 1
- grad_queries: bfloat16 [16, 98304, 128], P(None, ('dp', 'seq')), parts along dimension 1
- grad_keys: bfloat16 [16, 98304, 128], P(None, ('dp', 'seq')), parts along dimension 1
- grad_values: bfloat16 [16, 98304, 128], P(None, ('dp', 'seq')), parts along dimension 1
There are 8 independent parts, one for each index of `dp`. A program takes and returns all parts, laid end to end along the dimension named above; each array names one. Nothing has to cross between parts.
All inputs are finite; a program needn't handle non-finite values.
Results may differ from a plain program's by a relative error of at most 0.009.
Values may be sent and summed in bfloat16 or wider, within the bound.
A program may use at most 192 MiB of HBM per device.

v0:
```python
import jax
import jax.numpy as jnp
from jax import lax
from jax.sharding import PartitionSpec as P


def group_terms(pieces):
    q_blk, k_blk, v_blk, g_blk, pre_blk, suf_blk = pieces
    wide = jnp.float32
    length = q_blk.shape[1]
    rows_idx = jnp.arange(length, dtype=jnp.int32)
    causal = rows_idx[:, None] >= rows_idx[None, :]
    scores = jnp.einsum("htd,hsd->hts", q_blk, k_blk, preferred_element_type=wide)
    masked = jnp.where(causal[None], scores, 0.0).astype(jnp.bfloat16)
    dots = jnp.einsum("htd,hsd->hts", g_blk, v_blk, preferred_element_type=wide)
    mdots = jnp.where(causal[None], dots, 0.0).astype(jnp.bfloat16)
    inner = jnp.einsum("hts,hsd->htd", masked, v_blk, preferred_element_type=wide) + jnp.einsum(
        "hta,hab->htb", q_blk, pre_blk, preferred_element_type=wide
    )
    dq_full = jnp.einsum("hts,hsd->htd", mdots, k_blk, preferred_element_type=wide) + jnp.einsum(
        "htb,hab->hta", g_blk, pre_blk, preferred_element_type=wide
    )
    dk_full = jnp.einsum("hts,htd->hsd", mdots, q_blk, preferred_element_type=wide) + jnp.einsum(
        "hsb,hab->hsa", v_blk, suf_blk, preferred_element_type=wide
    )
    dv_full = jnp.einsum("hts,htd->hsd", masked, g_blk, preferred_element_type=wide) + jnp.einsum(
        "hsa,hab->hsb", k_blk, suf_blk, preferred_element_type=wide
    )
    return (
        inner,
        dq_full.astype(jnp.bfloat16),
        dk_full.astype(jnp.bfloat16),
        dv_full.astype(jnp.bfloat16),
    )


def on_device(queries, key_rows, value_rows, out_grad):
    wide = jnp.float32
    heads, length, width = queries.shape
    my_index = lax.axis_index("seq")
    count = lax.axis_size("seq")
    position = (my_index * length + jnp.arange(length, dtype=jnp.int32)).astype(wide)
    scale = 1.0 / jnp.sqrt(width * (position + 1.0))
    scaled_grad = (scale[None, :, None] * out_grad.astype(wide)).astype(jnp.bfloat16)
    key_state = jnp.einsum(
        "hta,htb->hab", key_rows, value_rows, preferred_element_type=wide
    ).astype(jnp.bfloat16)
    grad_state = jnp.einsum(
        "hta,htb->hab", queries, scaled_grad, preferred_element_type=wide
    ).astype(jnp.bfloat16)
    ranks = jnp.arange(count, dtype=jnp.int32)
    earlier = (ranks < my_index).astype(jnp.bfloat16)
    later = (ranks > my_index).astype(jnp.bfloat16)
    all_keys = lax.all_gather(key_state[None], "seq", axis=0, tiled=True)
    prefix = jnp.einsum("n,nhab->hab", earlier, all_keys, preferred_element_type=wide)
    all_grads = lax.all_gather(grad_state[None], "seq", axis=0, tiled=True)
    suffix = jnp.einsum("n,nhab->hab", later, all_grads, preferred_element_type=wide)
    prefix_half = prefix.astype(jnp.bfloat16)
    suffix_half = suffix.astype(jnp.bfloat16)
    group = 4
    steps_count = heads // group

    def grouped(array):
        return array.reshape((steps_count, group) + array.shape[1:])

    inner, grad_q, grad_k, grad_v = lax.map(
        group_terms,
        (
            grouped(queries),
            grouped(key_rows),
            grouped(value_rows),
            grouped(scaled_grad),
            grouped(prefix_half),
            grouped(suffix_half),
        ),
    )
    attended = (scale[None, :, None] * inner.reshape(heads, length, width)).astype(jnp.bfloat16)
    return (
        attended,
        grad_q.reshape(heads, length, width),
        grad_k.reshape(heads, length, width),
        grad_v.reshape(heads, length, width),
    )


def solution(mesh):
    placed = (
        P(None, ("dp", "seq"), None),
        P(None, ("dp", "seq"), None),
        P(None, ("dp", "seq"), None),
        P(None, ("dp", "seq"), None),
    )
    return jax.shard_map(
        on_device,
        mesh=mesh,
        in_specs=placed,
        out_specs=(
            P(None, ("dp", "seq"), None),
            P(None, ("dp", "seq"), None),
            P(None, ("dp", "seq"), None),
            P(None, ("dp", "seq"), None),
        ),
        check_vma=False,
    )
```

profile of v0, /device:TPU:1, one launch (start us, length us, event | category | flops | bytes accessed | tf_op | source)
XLA Modules:
  0.0 249.8 jit_solution(6098355292058006964)
XLA Ops:
  7.2 4.7 %convolution_convert_fusion.1 = bf16[16,128,128]{2,1,0:T(8,128)(2,1)} fusion(bf16[16,768,128]{2,1,0:T(8,128)(2,1)} %param.7, bf16[16,768,128]{2,1,0:T(8,128)(2,1)} %param.8), kind=kOutput, calls=%fused_computation.67 | convolution fusion | flops 402915328 | bytes 6815744 | tf_op jit(solution)/shard_map/hta,htb->hab/dot_general | solution.py:45
  12.0 2.9 %multiply_convert_fusion = bf16[16,768,128]{2,1,0:T(8,128)(2,1)S(1)} fusion(bf16[16,768,128]{2,1,0:T(8,128)(2,1)} %param.9, f32[768]{0:T(1024)S(1)} %multiply_rsqrt_fusion), kind=kLoop, calls=%fused_computation.65 | loop fusion | flops 4718592 | bytes 6294528 | tf_op jit(solution)/shard_map/convert_element_type | solution.py:44
  19.0 67.1 %all-gather.5.cloned.1.call-done = bf16[256,128,128]{2,1,0:T(8,128)(2,1)} async-done(((bf16[16,128,128]{2,1,0:T(8,128)(2,1)}), bf16[256,128,128]{2,1,0:T(8,128)(2,1)}) %all-gather.5.cloned.1.call-update) | async-done | bytes 8388624 | tf_op jit(solution)/shard_map/all_gather | solution.py:54
  86.1 8.3 %fusion.54 = f32[1,16,128,128]{3,0,2,1:T(1,128)S(1)} fusion(bf16[16,16,128,128]{3,2,1,0:T(8,128)(2,1)} %bitcast.143, s32[]{:T(128)S(6)} %axis_index.12), kind=kOutput, calls=%fused_computation.61 | convolution fusion | flops 8388624 | bytes 9437188 | tf_op jit(solution)/shard_map/n,nhab->hab/dot_general | solution.py:55
  95.2 63.5 %all-gather.7.cloned.1.call-done = bf16[256,128,128]{2,1,0:T(8,128)(2,1)} async-done(((bf16[16,128,128]{2,1,0:T(8,128)(2,1)}), bf16[256,128,128]{2,1,0:T(8,128)(2,1)}) %all-gather.7.cloned.1.call-update) | async-done | bytes 8388624 | tf_op jit(solution)/shard_map/all_gather | solution.py:56
  158.7 8.5 %fusion.52 = f32[1,16,128,128]{3,0,2,1:T(1,128)S(1)} fusion(bf16[16,16,128,128]{3,2,1,0:T(8,128)(2,1)} %bitcast.144, s32[]{:T(128)S(6)} %axis_index.12), kind=kOutput, calls=%fused_computation.59 | convolution fusion | flops 8388624 | bytes 9437188 | tf_op jit(solution)/shard_map/n,nhab->hab/dot_general | solution.py:57
  168.1 69.6 %while.16 = (s32[]{:T(128)}, f32[4,4,768,128]{3,2,1,0:T(8,128)}, bf16[4,4,768,128]{3,2,1,0:T(8,128)(2,1)}, bf16[4,4,768,128]{3,2,1,0:T(8,128)(2,1)}, bf16[4,4,76...) while((s32[]{:T(128)}, f32[4,4,768,128]{3,2,1,0:T(8,128)}, ...), condition=%wide.region_1.2_spmd, body=%wide.region_0.1_spmd.sunk | while | flops 4039311360 | bytes 96413928 | solution.py:66
  173.9 2.6 %fusion.125 = bf16[4,4,768,128]{3,2,1,0:T(8,128)(2,1)} fusion(bf16[4,4,768,128]{3,2,1,0:T(8,128)(2,1)} %get-tuple-element.172, s32[]{:T(128)S(6)} %copy.40, f32[4,768,128]{2,1,0:T(8,128)S(1)} %fusion.124, bf16[4,768,768]{2,1,0:T(8,128)(2,1)S(1)} %select_convert_fusion.5, bf16[4,4,768,128]{3,2,1,0:T(8,128)(2,1)S(1)} %copy-done.1), kind=kOutput, calls=%fused_computation.10.clone.1 | convolution fusion | flops 604766208 | bytes 7865344 | tf_op jit(solution)/shard_map/while/body/eval_jaxpr/hts,htd->hsd/dot_general | solution.py:23
  176.5 2.3 fusion.123
  180.3 2.6 %fusion.127 = bf16[4,4,768,128]{3,2,1,0:T(8,128)(2,1)} fusion(bf16[4,4,768,128]{3,2,1,0:T(8,128)(2,1)} %get-tuple-element.173, s32[]{:T(128)S(6)} %copy.40, f32[4,768,128]{2,1,0:T(8,128)S(1)} %fusion.126, bf16[4,768,768]{2,1,0:T(8,128)(2,1)S(1)} %select_convert_fusion.4, bf16[4,4,768,128]{3,2,1,0:T(8,128)(2,1)S(1)} %get-tuple-element.190), kind=kOutput, calls=%fused_computation.12.clone.1 | convolution fusion | flops 604766208 | bytes 7865344 | tf_op jit(solution)/shard_map/while/body/eval_jaxpr/hts,htd->hsd/dot_general | solution.py:26
  182.9 2.6 %bitcast_dynamic-update-slice_fusion.2 = f32[4,4,768,128]{3,2,1,0:T(8,128)} fusion(f32[4,4,768,128]{3,2,1,0:T(8,128)} %get-tuple-element.170, s32[]{:T(128)S(6)} %copy.40, f32[4,768,128]{2,1,0:T(8,128)S(1)} %fusion.121, bf16[4,768,768]{2,1,0:T(8,128)(2,1)S(1)} %select_convert_fusion.4, bf16[4,4,768,128]{3,2,1,0:T(8,128)(2,1)S(1)} %copy-done.2), kind=kOutput, calls=%fused_computation.3.clone.1 | convolution fusion | flops 604372992 | bytes 8651776 | tf_op jit(solution)/shard_map/while/body/eval_jaxpr/hts,hsd->htd/dot_general | solution.py:17
  191.3 2.6 %fusion.125 = bf16[4,4,768,128]{3,2,1,0:T(8,128)(2,1)} fusion(bf16[4,4,768,128]{3,2,1,0:T(8,128)(2,1)} %get-tuple-element.172, s32[]{:T(128)S(6)} %copy.40, f32[4,768,128]{2,1,0:T(8,128)S(1)} %fusion.124, bf16[4,768,768]{2,1,0:T(8,128)(2,1)S(1)} %select_convert_fusion.5, bf16[4,4,768,128]{3,2,1,0:T(8,128)(2,1)S(1)} %copy-done.1), kind=kOutput, calls=%fused_computation.10.clone.1 | convolution fusion | flops 604766208 | bytes 7865344 | tf_op jit(solution)/shard_map/while/body/eval_jaxpr/hts,htd->hsd/dot_general | solution.py:23
  193.9 2.3 fusion.123
  197.7 2.6 %fusion.127 = bf16[4,4,768,128]{3,2,1,0:T(8,128)(2,1)} fusion(bf16[4,4,768,128]{3,2,1,0:T(8,128)(2,1)} %get-tuple-element.173, s32[]{:T(128)S(6)} %copy.40, f32[4,768,128]{2,1,0:T(8,128)S(1)} %fusion.126, bf16[4,768,768]{2,1,0:T(8,128)(2,1)S(1)} %select_convert_fusion.4, bf16[4,4,768,128]{3,2,1,0:T(8,128)(2,1)S(1)} %get-tuple-element.190), kind=kOutput, calls=%fused_computation.12.clone.1 | convolution fusion | flops 604766208 | bytes 7865344 | tf_op jit(solution)/shard_map/while/body/eval_jaxpr/hts,htd->hsd/dot_general | solution.py:26
  200.3 2.6 %bitcast_dynamic-update-slice_fusion.2 = f32[4,4,768,128]{3,2,1,0:T(8,128)} fusion(f32[4,4,768,128]{3,2,1,0:T(8,128)} %get-tuple-element.170, s32[]{:T(128)S(6)} %copy.40, f32[4,768,128]{2,1,0:T(8,128)S(1)} %fusion.121, bf16[4,768,768]{2,1,0:T(8,128)(2,1)S(1)} %select_convert_fusion.4, bf16[4,4,768,128]{3,2,1,0:T(8,128)(2,1)S(1)} %copy-done.2), kind=kOutput, calls=%fused_computation.3.clone.1 | convolution fusion | flops 604372992 | bytes 8651776 | tf_op jit(solution)/shard_map/while/body/eval_jaxpr/hts,hsd->htd/dot_general | solution.py:17
  208.7 2.6 %fusion.125 = bf16[4,4,768,128]{3,2,1,0:T(8,128)(2,1)} fusion(bf16[4,4,768,128]{3,2,1,0:T(8,128)(2,1)} %get-tuple-element.172, s32[]{:T(128)S(6)} %copy.40, f32[4,768,128]{2,1,0:T(8,128)S(1)} %fusion.124, bf16[4,768,768]{2,1,0:T(8,128)(2,1)S(1)} %select_convert_fusion.5, bf16[4,4,768,128]{3,2,1,0:T(8,128)(2,1)S(1)} %copy-done.1), kind=kOutput, calls=%fused_computation.10.clone.1 | convolution fusion | flops 604766208 | bytes 7865344 | tf_op jit(solution)/shard_map/while/body/eval_jaxpr/hts,htd->hsd/dot_general | solution.py:23
  211.3 2.3 fusion.123
  215.1 2.6 %fusion.127 = bf16[4,4,768,128]{3,2,1,0:T(8,128)(2,1)} fusion(bf16[4,4,768,128]{3,2,1,0:T(8,128)(2,1)} %get-tuple-element.173, s32[]{:T(128)S(6)} %copy.40, f32[4,768,128]{2,1,0:T(8,128)S(1)} %fusion.126, bf16[4,768,768]{2,1,0:T(8,128)(2,1)S(1)} %select_convert_fusion.4, bf16[4,4,768,128]{3,2,1,0:T(8,128)(2,1)S(1)} %get-tuple-element.190), kind=kOutput, calls=%fused_computation.12.clone.1 | convolution fusion | flops 604766208 | bytes 7865344 | tf_op jit(solution)/shard_map/while/body/eval_jaxpr/hts,htd->hsd/dot_general | solution.py:26
  217.7 2.6 %bitcast_dynamic-update-slice_fusion.2 = f32[4,4,768,128]{3,2,1,0:T(8,128)} fusion(f32[4,4,768,128]{3,2,1,0:T(8,128)} %get-tuple-element.170, s32[]{:T(128)S(6)} %copy.40, f32[4,768,128]{2,1,0:T(8,128)S(1)} %fusion.121, bf16[4,768,768]{2,1,0:T(8,128)(2,1)S(1)} %select_convert_fusion.4, bf16[4,4,768,128]{3,2,1,0:T(8,128)(2,1)S(1)} %copy-done.2), kind=kOutput, calls=%fused_computation.3.clone.1 | convolution fusion | flops 604372992 | bytes 8651776 | tf_op jit(solution)/shard_map/while/body/eval_jaxpr/hts,hsd->htd/dot_general | solution.py:17
  226.1 2.6 %fusion.125 = bf16[4,4,768,128]{3,2,1,0:T(8,128)(2,1)} fusion(bf16[4,4,768,128]{3,2,1,0:T(8,128)(2,1)} %get-tuple-element.172, s32[]{:T(128)S(6)} %copy.40, f32[4,768,128]{2,1,0:T(8,128)S(1)} %fusion.124, bf16[4,768,768]{2,1,0:T(8,128)(2,1)S(1)} %select_convert_fusion.5, bf16[4,4,768,128]{3,2,1,0:T(8,128)(2,1)S(1)} %copy-done.1), kind=kOutput, calls=%fused_computation.10.clone.1 | convolution fusion | flops 604766208 | bytes 7865344 | tf_op jit(solution)/shard_map/while/body/eval_jaxpr/hts,htd->hsd/dot_general | solution.py:23
  228.7 2.3 fusion.123
  232.5 2.6 %fusion.127 = bf16[4,4,768,128]{3,2,1,0:T(8,128)(2,1)} fusion(bf16[4,4,768,128]{3,2,1,0:T(8,128)(2,1)} %get-tuple-element.173, s32[]{:T(128)S(6)} %copy.40, f32[4,768,128]{2,1,0:T(8,128)S(1)} %fusion.126, bf16[4,768,768]{2,1,0:T(8,128)(2,1)S(1)} %select_convert_fusion.4, bf16[4,4,768,128]{3,2,1,0:T(8,128)(2,1)S(1)} %get-tuple-element.190), kind=kOutput, calls=%fused_computation.12.clone.1 | convolution fusion | flops 604766208 | bytes 7865344 | tf_op jit(solution)/shard_map/while/body/eval_jaxpr/hts,htd->hsd/dot_general | solution.py:26
  235.1 2.6 %bitcast_dynamic-update-slice_fusion.2 = f32[4,4,768,128]{3,2,1,0:T(8,128)} fusion(f32[4,4,768,128]{3,2,1,0:T(8,128)} %get-tuple-element.170, s32[]{:T(128)S(6)} %copy.40, f32[4,768,128]{2,1,0:T(8,128)S(1)} %fusion.121, bf16[4,768,768]{2,1,0:T(8,128)(2,1)S(1)} %select_convert_fusion.4, bf16[4,4,768,128]{3,2,1,0:T(8,128)(2,1)S(1)} %copy-done.2), kind=kOutput, calls=%fused_computation.3.clone.1 | convolution fusion | flops 604372992 | bytes 8651776 | tf_op jit(solution)/shard_map/while/body/eval_jaxpr/hts,hsd->htd/dot_general | solution.py:17
  237.7 5.2 %fusion.56 = bf16[16,768,128]{2,1,0:T(8,128)(2,1)} fusion(f32[4,4,768,128]{3,2,1,0:T(8,128)} %get-tuple-element.64, f32[768]{0:T(1024)S(1)} %multiply_rsqrt_fusion), kind=kLoop, calls=%fused_computation.64 | loop fusion | flops 3145728 | bytes 9440256 | tf_op jit(solution)/shard_map/convert_element_type | solution.py:77
  (75 shorter events, 34.7 us)
Async XLA Ops:
  7.2 78.9 %all-gather.5.cloned.1.call-start = ((), (), s32[]{:S(2)}) async-start(), calls=%async_computation | async-start | bytes 8912896 | tf_op jit(solution)/shard_map/all_gather | solution.py:54
  11.9 146.8 %all-gather.7.cloned.1.call-start = ((), (), s32[]{:S(2)}) async-start(), calls=%async_computation.1 | async-start | bytes 8912896 | tf_op jit(solution)/shard_map/all_gather | solution.py:56
  12.0 3.0 %copy-start = (bf16[16,768,128]{2,1,0:T(8,128)(2,1)S(1)}, bf16[16,768,128]{2,1,0:T(8,128)(2,1)}, u32[]{:S(2)}) copy-start(bf16[16,768,128]{2,1,0:T(8,128)(2,1)} %param.6) | copy-start | bytes 9437188
  168.1 3.5 %copy-start.1 = (bf16[4,4,768,128]{3,2,1,0:T(8,128)(2,1)S(1)}, bf16[4,4,768,128]{3,2,1,0:T(8,128)(2,1)}, u32[]{:S(2)}) copy-start(bf16[4,4,768,128]{3,2,1,0:T(8,128)(2,1)} %get-tuple-element.186) | copy-start | bytes 9437188 | tf_op jit(solution)/shard_map/while
  168.1 3.5 %copy-start.4 = (bf16[4,4,128,128]{3,2,1,0:T(8,128)(2,1)S(1)}, bf16[4,4,128,128]{3,2,1,0:T(8,128)(2,1)}, u32[]{:S(2)}) copy-start(bf16[4,4,128,128]{3,2,1,0:T(8,128)(2,1)} %get-tuple-element.189) | copy-start | bytes 1572868 | tf_op jit(solution)/shard_map/while
  170.0 2.4 copy-start.2
  173.9 2.6 %copy-start.3 = (bf16[4,4,768,128]{3,2,1,0:T(8,128)(2,1)S(1)}, bf16[4,4,768,128]{3,2,1,0:T(8,128)(2,1)}, u32[]{:S(2)}) copy-start(bf16[4,4,768,128]{3,2,1,0:T(8,128)(2,1)} %get-tuple-element.187) | copy-start | bytes 9437188 | tf_op jit(solution)/shard_map/while
  185.5 3.5 %copy-start.1 = (bf16[4,4,768,128]{3,2,1,0:T(8,128)(2,1)S(1)}, bf16[4,4,768,128]{3,2,1,0:T(8,128)(2,1)}, u32[]{:S(2)}) copy-start(bf16[4,4,768,128]{3,2,1,0:T(8,128)(2,1)} %get-tuple-element.186) | copy-start | bytes 9437188 | tf_op jit(solution)/shard_map/while
  185.5 3.5 %copy-start.4 = (bf16[4,4,128,128]{3,2,1,0:T(8,128)(2,1)S(1)}, bf16[4,4,128,128]{3,2,1,0:T(8,128)(2,1)}, u32[]{:S(2)}) copy-start(bf16[4,4,128,128]{3,2,1,0:T(8,128)(2,1)} %get-tuple-element.189) | copy-start | bytes 1572868 | tf_op jit(solution)/shard_map/while
  187.3 2.4 copy-start.2
  191.3 2.6 %copy-start.3 = (bf16[4,4,768,128]{3,2,1,0:T(8,128)(2,1)S(1)}, bf16[4,4,768,128]{3,2,1,0:T(8,128)(2,1)}, u32[]{:S(2)}) copy-start(bf16[4,4,768,128]{3,2,1,0:T(8,128)(2,1)} %get-tuple-element.187) | copy-start | bytes 9437188 | tf_op jit(solution)/shard_map/while
  202.9 3.5 %copy-start.1 = (bf16[4,4,768,128]{3,2,1,0:T(8,128)(2,1)S(1)}, bf16[4,4,768,128]{3,2,1,0:T(8,128)(2,1)}, u32[]{:S(2)}) copy-start(bf16[4,4,768,128]{3,2,1,0:T(8,128)(2,1)} %get-tuple-element.186) | copy-start | bytes 9437188 | tf_op jit(solution)/shard_map/while
  202.9 3.5 %copy-start.4 = (bf16[4,4,128,128]{3,2,1,0:T(8,128)(2,1)S(1)}, bf16[4,4,128,128]{3,2,1,0:T(8,128)(2,1)}, u32[]{:S(2)}) copy-start(bf16[4,4,128,128]{3,2,1,0:T(8,128)(2,1)} %get-tuple-element.189) | copy-start | bytes 1572868 | tf_op jit(solution)/shard_map/while
  204.7 2.4 copy-start.2
  208.7 2.6 %copy-start.3 = (bf16[4,4,768,128]{3,2,1,0:T(8,128)(2,1)S(1)}, bf16[4,4,768,128]{3,2,1,0:T(8,128)(2,1)}, u32[]{:S(2)}) copy-start(bf16[4,4,768,128]{3,2,1,0:T(8,128)(2,1)} %get-tuple-element.187) | copy-start | bytes 9437188 | tf_op jit(solution)/shard_map/while
  220.3 3.5 %copy-start.1 = (bf16[4,4,768,128]{3,2,1,0:T(8,128)(2,1)S(1)}, bf16[4,4,768,128]{3,2,1,0:T(8,128)(2,1)}, u32[]{:S(2)}) copy-start(bf16[4,4,768,128]{3,2,1,0:T(8,128)(2,1)} %get-tuple-element.186) | copy-start | bytes 9437188 | tf_op jit(solution)/shard_map/while
  220.3 3.5 %copy-start.4 = (bf16[4,4,128,128]{3,2,1,0:T(8,128)(2,1)S(1)}, bf16[4,4,128,128]{3,2,1,0:T(8,128)(2,1)}, u32[]{:S(2)}) copy-start(bf16[4,4,128,128]{3,2,1,0:T(8,128)(2,1)} %get-tuple-element.189) | copy-start | bytes 1572868 | tf_op jit(solution)/shard_map/while
  222.1 2.4 copy-start.2
  226.1 2.6 %copy-start.3 = (bf16[4,4,768,128]{3,2,1,0:T(8,128)(2,1)S(1)}, bf16[4,4,768,128]{3,2,1,0:T(8,128)(2,1)}, u32[]{:S(2)}) copy-start(bf16[4,4,768,128]{3,2,1,0:T(8,128)(2,1)} %get-tuple-element.187) | copy-start | bytes 9437188 | tf_op jit(solution)/shard_map/while
Sparse Core Ops, SparseCore 0:
  12.1 73.9 all-gather.4
  88.2 70.4 all-gather.6
where the time goes:
time: 250 us
  waiting for transfers between devices  131 us (52%)
  matrix products  91.8 us (37%)
  between operations  14.1 us (6%)
  other arithmetic  10.7 us (4%)
    all_gather x1, waiting for transfers between devices, on_device(): all_keys = lax.all_gather(key_state[None], 'seq', axis=0, tiled=True)  67.1 us
    all_gather x1, waiting for transfers between devices, on_device(): all_grads = lax.all_gather(grad_state[None], 'seq', axis=0, tiled=True)  63.5 us
    dot_general x4, matrix products, group_terms(): jnp.einsum('hts,htd->hsd', masked, g_blk, preferred_element_type=wide)  10.5 us
    dot_general x4, matrix products, group_terms(): jnp.einsum('hts,htd->hsd', mdots, q_blk, preferred_element_type=wide)  10.4 us
    dot_general x4, matrix products, group_terms(): jnp.einsum('hts,hsd->htd', masked, v_blk, preferred_element_type=wide)  10.3 us
    dot_general x4, matrix products, group_terms(): jnp.einsum('hts,hsd->htd', mdots, k_blk, preferred_element_type=wide)  9.14 us
    dot_general x1, matrix products, on_device(): jnp.einsum('n,nhab->hab', later, all_grads, preferred_element_type=wide)  8.47 us
    dot_general x1, matrix products, on_device(): jnp.einsum('n,nhab->hab', earlier, all_keys, preferred_element_type=wide)  8.3 us
  transfers between devices with their start and end apart: 2, of which 2 were waited for; matrix products, arithmetic and copies ran while one was open for 6% of the time, Pallas kernels for 0%

commit v1 on v0

--- a/solution.py
+++ b/solution.py
@@ -53,7 +53,9 @@
     later = (ranks > my_index).astype(jnp.bfloat16)
     all_keys = lax.all_gather(key_state[None], "seq", axis=0, tiled=True)
     prefix = jnp.einsum("n,nhab->hab", earlier, all_keys, preferred_element_type=wide)
-    all_grads = lax.all_gather(grad_state[None], "seq", axis=0, tiled=True)
+    all_grads = jnp.concatenate(
+        lax.all_to_all(jnp.stack([grad_state[None]] * lax.axis_size("seq")), "seq", 0, 0), axis=0
+    )
     suffix = jnp.einsum("n,nhab->hab", later, all_grads, preferred_element_type=wide)
     prefix_half = prefix.astype(jnp.bfloat16)
     suffix_half = suffix.astype(jnp.bfloat16)

time: 250 us -> 293 us (1.17)
  waiting for transfers between devices: 131 us -> 162 us
  starting transfers between devices: 0.08 us -> 8.75 us
  local copies, waits for them, and re-layouts: 2.15 us -> 8.88 us
  matrix products: 91.8 us -> 87.8 us
    all_to_all x0 -> x1, waiting for transfers between devices: none -> 162 us  [on_device(): lax.all_to_all(jnp.stack([grad_state[None]] * lax.axis_size('seq')), 'seq...]
    all_gather x1, waiting for transfers between devices: 67.1 us -> 0.01 us  [on_device(): all_keys = lax.all_gather(key_state[None], 'seq', axis=0, tiled=True)]
    all_gather x1 -> x0, waiting for transfers between devices: 63.5 us -> none  [on_device(): all_grads = lax.all_gather(grad_state[None], 'seq', axis=0, tiled=True)]
    all_to_all x0 -> x1, starting transfers between devices: none -> 8.71 us  [on_device(): lax.all_to_all(jnp.stack([grad_state[None]] * lax.axis_size('seq')), 'seq...]
    another operation x0 -> x1, local copies, waits for them, and re-layouts: none -> 6.39 us  [on_device(): jnp.stack([grad_state[None]] * lax.axis_size('seq'))]
    dot_general x4, matrix products: 5.96 us -> 12 us  [group_terms(): jnp.einsum('htd,hsd->hts', q_blk, k_blk, preferred_element_type=wide)]
    dot_general x4, matrix products: 6.59 us -> 1.39 us  [group_terms(): jnp.einsum('hsa,hab->hsb', k_blk, suf_blk, preferred_element_type=wide)]
    dot_general x4, matrix products: 6.64 us -> 1.47 us  [group_terms(): jnp.einsum('hsb,hab->hsa', v_blk, suf_blk, preferred_element_type=wide)]
  transfers between devices with their start and end apart: 2 -> 2, of which waited for: 2 -> 1; matrix products, arithmetic and copies ran while one was open for 6% -> 8% of each run, Pallas kernels for 0% -> 0%
where the time goes in v1:
time: 293 us; the launch traced here: 292 us
  waiting for transfers between devices  162 us (55%)
  matrix products  87.8 us (30%)
  between operations  14.1 us (5%)
  other arithmetic  10.7 us (4%)
  local copies, waits for them, and re-layouts  8.88 us (3%)
  starting transfers between devices  8.75 us (3%)
    all_to_all x1, waiting for transfers between devices, on_device(): lax.all_to_all(jnp.stack([grad_state[None]] * lax.axis_size('seq')), 'seq...  162 us
    dot_general x4, matrix products, group_terms(): jnp.einsum('htd,hsd->hts', q_blk, k_blk, preferred_element_type=wide)  12 us
    dot_general x4, matrix products, group_terms(): jnp.einsum('hts,hsd->htd', masked, v_blk, preferred_element_type=wide)  10.6 us
    dot_general x4, matrix products, group_terms(): jnp.einsum('hts,htd->hsd', masked, g_blk, preferred_element_type=wide)  10.5 us
    dot_general x4, matrix products, group_terms(): jnp.einsum('hts,htd->hsd', mdots, q_blk, preferred_element_type=wide)  10.4 us
    dot_general x4, matrix products, group_terms(): jnp.einsum('hts,hsd->htd', mdots, k_blk, preferred_element_type=wide)  9.4 us
    all_to_all x1, starting transfers between devices, on_device(): lax.all_to_all(jnp.stack([grad_state[None]] * lax.axis_size('seq')), 'seq...  8.71 us
    dot_general x1, matrix products, on_device(): jnp.einsum('n,nhab->hab', earlier, all_keys, preferred_element_type=wide)  8.3 us
  transfers between devices with their start and end apart: 2, of which 1 were waited for; matrix products, arithmetic and copies ran while one was open for 8% of the time, Pallas kernels for 0%

profile of v1, /device:TPU:1, one launch (start us, length us, event | category | flops | bytes accessed | tf_op | source)
XLA Modules:
  0.0 292.5 jit_solution(8878645797561867769)
XLA Ops:
  7.2 4.7 %convolution_convert_fusion.1 = bf16[16,128,128]{2,1,0:T(8,128)(2,1)} fusion(bf16[16,768,128]{2,1,0:T(8,128)(2,1)} %param.7, bf16[16,768,128]{2,1,0:T(8,128)(2,1)} %param.8), kind=kOutput, calls=%fused_computation.67 | convolution fusion | flops 402915328 | bytes 6815744 | tf_op jit(solution)/shard_map/hta,htb->hab/dot_general | solution.py:45
  12.0 2.9 %multiply_convert_fusion = bf16[16,768,128]{2,1,0:T(8,128)(2,1)S(1)} fusion(bf16[16,768,128]{2,1,0:T(8,128)(2,1)} %param.9, f32[768]{0:T(1024)S(1)} %multiply_rsqrt_fusion), kind=kLoop, calls=%fused_computation.65 | loop fusion | flops 4718592 | bytes 6294528 | tf_op jit(solution)/shard_map/convert_element_type | solution.py:44
  18.9 6.4 %stack.3 = bf16[16,1,16,128,128]{4,3,2,1,0:T(8,128)(2,1)} broadcast(bf16[16,128,128]{2,1,0:T(8,128)(2,1)} %copy.17), dimensions={2,3,4} | broadcast | bytes 8912896 | tf_op jit(solution)/shard_map/stack | solution.py:57
  25.3 8.7 %all-to-all-start = ((bf16[16,1,16,128,128]{4,3,2,1,0:T(8,128)(2,1)}), bf16[16,1,16,128,128]{4,3,2,1,0:T(8,128)(2,1)}, u32[]{:S(2)}, u32[]{:S(2)}) async-start(bf16[16,1,16,128,128]{4,3,2,1,0:T(8,128)(2,1)} %stack.3), calls=%async_computation | async-start | bytes 16777216 | tf_op jit(solution)/shard_map/all_to_all | solution.py:57
  34.0 161.9 %all-to-all-done = bf16[16,1,16,128,128]{4,3,2,1,0:T(8,128)(2,1)} async-done(((bf16[16,1,16,128,128]{4,3,2,1,0:T(8,128)(2,1)}), bf16[16,1,16,128,128]{4,3,2,1,0:T(8,128)(2,1)}, u32[]{:S(2)}, u32[]{:S(2)}) %all-to-all-start) | async-done | bytes 8388640 | tf_op jit(solution)/shard_map/all_to_all | solution.py:57
  195.9 8.3 %fusion.52 = f32[1,16,128,128]{3,0,2,1:T(1,128)S(1)} fusion(bf16[16,16,128,128]{3,2,1,0:T(8,128)(2,1)} %bitcast.23, s32[]{:T(128)S(6)} %axis_index.12), kind=kOutput, calls=%fused_computation.59 | convolution fusion | flops 8388624 | bytes 9437188 | tf_op jit(solution)/shard_map/n,nhab->hab/dot_general | solution.py:59
  205.1 8.3 %fusion.54 = f32[1,16,128,128]{3,0,2,1:T(1,128)S(1)} fusion(bf16[16,16,128,128]{3,2,1,0:T(8,128)(2,1)} %bitcast.143, s32[]{:T(128)S(6)} %axis_index.12), kind=kOutput, calls=%fused_computation.61 | convolution fusion | flops 8388624 | bytes 9437188 | tf_op jit(solution)/shard_map/n,nhab->hab/dot_general | solution.py:55
  214.3 66.1 %while.16 = (s32[]{:T(128)}, f32[4,4,768,128]{3,2,1,0:T(8,128)}, bf16[4,4,768,128]{3,2,1,0:T(8,128)(2,1)}, bf16[4,4,768,128]{3,2,1,0:T(8,128)(2,1)}, bf16[4,4,76...) while((s32[]{:T(128)}, f32[4,4,768,128]{3,2,1,0:T(8,128)}, ...), condition=%wide.region_1.2_spmd, body=%wide.region_0.1_spmd.sunk | while | flops 4039311360 | bytes 98511104 | solution.py:68
  214.5 3.0 %select_convert_fusion.4 = bf16[4,768,768]{2,1,0:T(8,128)(2,1)S(1)} fusion(pred[768,768]{1,0:T(8,128)(4,1)S(1)} %iota_compare_fusion.2, bf16[4,4,768,128]{3,2,1,0:T(8,128)(2,1)} %get-tuple-element.187, s32[]{:T(128)} %get-tuple-element.169, bf16[4,4,768,128]{3,2,1,0:T(8,128)(2,1)} %get-tuple-element.186), kind=kOutput, calls=%fused_computation.1.clone.1 | convolution fusion | flops 608698368 | bytes 6882304 | tf_op jit(solution)/shard_map/while/body/eval_jaxpr/htd,hsd->hts/dot_general | solution.py:13
  218.0 2.7 bitcast_dynamic-update-slice_fusion.2
  225.2 2.6 fusion.125
  228.2 2.6 fusion.127
  231.0 3.0 %select_convert_fusion.4 = bf16[4,768,768]{2,1,0:T(8,128)(2,1)S(1)} fusion(pred[768,768]{1,0:T(8,128)(4,1)S(1)} %iota_compare_fusion.2, bf16[4,4,768,128]{3,2,1,0:T(8,128)(2,1)} %get-tuple-element.187, s32[]{:T(128)} %get-tuple-element.169, bf16[4,4,768,128]{3,2,1,0:T(8,128)(2,1)} %get-tuple-element.186), kind=kOutput, calls=%fused_computation.1.clone.1 | convolution fusion | flops 608698368 | bytes 6882304 | tf_op jit(solution)/shard_map/while/body/eval_jaxpr/htd,hsd->hts/dot_general | solution.py:13
  234.5 2.6 bitcast_dynamic-update-slice_fusion.2
  241.7 2.6 fusion.125
  244.7 2.6 fusion.127
  247.5 3.0 %select_convert_fusion.4 = bf16[4,768,768]{2,1,0:T(8,128)(2,1)S(1)} fusion(pred[768,768]{1,0:T(8,128)(4,1)S(1)} %iota_compare_fusion.2, bf16[4,4,768,128]{3,2,1,0:T(8,128)(2,1)} %get-tuple-element.187, s32[]{:T(128)} %get-tuple-element.169, bf16[4,4,768,128]{3,2,1,0:T(8,128)(2,1)} %get-tuple-element.186), kind=kOutput, calls=%fused_computation.1.clone.1 | convolution fusion | flops 608698368 | bytes 6882304 | tf_op jit(solution)/shard_map/while/body/eval_jaxpr/htd,hsd->hts/dot_general | solution.py:13
  251.0 2.7 bitcast_dynamic-update-slice_fusion.2
  258.3 2.6 fusion.125
  261.2 2.6 fusion.127
  264.1 3.0 %select_convert_fusion.4 = bf16[4,768,768]{2,1,0:T(8,128)(2,1)S(1)} fusion(pred[768,768]{1,0:T(8,128)(4,1)S(1)} %iota_compare_fusion.2, bf16[4,4,768,128]{3,2,1,0:T(8,128)(2,1)} %get-tuple-element.187, s32[]{:T(128)} %get-tuple-element.169, bf16[4,4,768,128]{3,2,1,0:T(8,128)(2,1)} %get-tuple-element.186), kind=kOutput, calls=%fused_computation.1.clone.1 | convolution fusion | flops 608698368 | bytes 6882304 | tf_op jit(solution)/shard_map/while/body/eval_jaxpr/htd,hsd->hts/dot_general | solution.py:13
  267.5 2.6 bitcast_dynamic-update-slice_fusion.2
  277.7 2.6 fusion.127
  280.4 5.2 %fusion.56 = bf16[16,768,128]{2,1,0:T(8,128)(2,1)} fusion(f32[4,4,768,128]{3,2,1,0:T(8,128)} %get-tuple-element.64, f32[768]{0:T(1024)S(1)} %multiply_rsqrt_fusion), kind=kLoop, calls=%fused_computation.64 | loop fusion | flops 3145728 | bytes 9440256 | tf_op jit(solution)/shard_map/convert_element_type | solution.py:79
  (83 shorter events, 30.7 us)
Async XLA Ops:
  7.2 197.9 %all-gather.3.cloned.1.call-start = ((), (), s32[]{:S(2)}) async-start(), calls=%async_computation.1 | async-start | bytes 8912896 | tf_op jit(solution)/shard_map/all_gather | solution.py:54
  12.0 3.0 %copy-start = (bf16[16,768,128]{2,1,0:T(8,128)(2,1)S(1)}, bf16[16,768,128]{2,1,0:T(8,128)(2,1)}, u32[]{:S(2)}) copy-start(bf16[16,768,128]{2,1,0:T(8,128)(2,1)} %param.6) | copy-start | bytes 9437188
  25.3 170.6 %all-to-all-start = ((bf16[16,1,16,128,128]{4,3,2,1,0:T(8,128)(2,1)}), bf16[16,1,16,128,128]{4,3,2,1,0:T(8,128)(2,1)}, u32[]{:S(2)}, u32[]{:S(2)}) async-start(bf16[16,1,16,128,128]{4,3,2,1,0:T(8,128)(2,1)} %stack.3), calls=%async_computation | async-start | bytes 16777216 | tf_op jit(solution)/shard_map/all_to_all | solution.py:57
  214.5 3.0 %copy-start.1 = (bf16[4,4,768,128]{3,2,1,0:T(8,128)(2,1)S(1)}, bf16[4,4,768,128]{3,2,1,0:T(8,128)(2,1)}, u32[]{:S(2)}) copy-start(bf16[4,4,768,128]{3,2,1,0:T(8,128)(2,1)} %get-tuple-element.186) | copy-start | bytes 9437188 | tf_op jit(solution)/shard_map/while
  214.5 3.0 %copy-start.5 = (bf16[4,4,128,128]{3,2,1,0:T(8,128)(2,1)S(1)}, bf16[4,4,128,128]{3,2,1,0:T(8,128)(2,1)}, u32[]{:S(2)}) copy-start(bf16[4,4,128,128]{3,2,1,0:T(8,128)(2,1)} %get-tuple-element.189) | copy-start | bytes 1572868 | tf_op jit(solution)/shard_map/while
  214.5 3.5 %copy-start.2 = (bf16[4,4,768,128]{3,2,1,0:T(8,128)(2,1)S(1)}, bf16[4,4,768,128]{3,2,1,0:T(8,128)(2,1)}, u32[]{:S(2)}) copy-start(bf16[4,4,768,128]{3,2,1,0:T(8,128)(2,1)} %get-tuple-element.188) | copy-start | bytes 9437188 | tf_op jit(solution)/shard_map/while
  220.6 1.9 copy-start.3
  222.5 2.4 copy-start.4
  231.0 3.0 %copy-start.1 = (bf16[4,4,768,128]{3,2,1,0:T(8,128)(2,1)S(1)}, bf16[4,4,768,128]{3,2,1,0:T(8,128)(2,1)}, u32[]{:S(2)}) copy-start(bf16[4,4,768,128]{3,2,1,0:T(8,128)(2,1)} %get-tuple-element.186) | copy-start | bytes 9437188 | tf_op jit(solution)/shard_map/while
  231.0 3.0 %copy-start.5 = (bf16[4,4,128,128]{3,2,1,0:T(8,128)(2,1)S(1)}, bf16[4,4,128,128]{3,2,1,0:T(8,128)(2,1)}, u32[]{:S(2)}) copy-start(bf16[4,4,128,128]{3,2,1,0:T(8,128)(2,1)} %get-tuple-element.189) | copy-start | bytes 1572868 | tf_op jit(solution)/shard_map/while
  231.0 3.5 %copy-start.2 = (bf16[4,4,768,128]{3,2,1,0:T(8,128)(2,1)S(1)}, bf16[4,4,768,128]{3,2,1,0:T(8,128)(2,1)}, u32[]{:S(2)}) copy-start(bf16[4,4,768,128]{3,2,1,0:T(8,128)(2,1)} %get-tuple-element.188) | copy-start | bytes 9437188 | tf_op jit(solution)/shard_map/while
  237.1 1.9 copy-start.3
  239.0 2.4 copy-start.4
  247.5 3.0 %copy-start.1 = (bf16[4,4,768,128]{3,2,1,0:T(8,128)(2,1)S(1)}, bf16[4,4,768,128]{3,2,1,0:T(8,128)(2,1)}, u32[]{:S(2)}) copy-start(bf16[4,4,768,128]{3,2,1,0:T(8,128)(2,1)} %get-tuple-element.186) | copy-start | bytes 9437188 | tf_op jit(solution)/shard_map/while
  247.5 3.0 %copy-start.5 = (bf16[4,4,128,128]{3,2,1,0:T(8,128)(2,1)S(1)}, bf16[4,4,128,128]{3,2,1,0:T(8,128)(2,1)}, u32[]{:S(2)}) copy-start(bf16[4,4,128,128]{3,2,1,0:T(8,128)(2,1)} %get-tuple-element.189) | copy-start | bytes 1572868 | tf_op jit(solution)/shard_map/while
  247.5 3.5 %copy-start.2 = (bf16[4,4,768,128]{3,2,1,0:T(8,128)(2,1)S(1)}, bf16[4,4,768,128]{3,2,1,0:T(8,128)(2,1)}, u32[]{:S(2)}) copy-start(bf16[4,4,768,128]{3,2,1,0:T(8,128)(2,1)} %get-tuple-element.188) | copy-start | bytes 9437188 | tf_op jit(solution)/shard_map/while
  253.7 1.9 copy-start.3
  255.6 2.4 copy-start.4
  264.0 3.0 %copy-start.1 = (bf16[4,4,768,128]{3,2,1,0:T(8,128)(2,1)S(1)}, bf16[4,4,768,128]{3,2,1,0:T(8,128)(2,1)}, u32[]{:S(2)}) copy-start(bf16[4,4,768,128]{3,2,1,0:T(8,128)(2,1)} %get-tuple-element.186) | copy-start | bytes 9437188 | tf_op jit(solution)/shard_map/while
  264.1 3.0 %copy-start.5 = (bf16[4,4,128,128]{3,2,1,0:T(8,128)(2,1)S(1)}, bf16[4,4,128,128]{3,2,1,0:T(8,128)(2,1)}, u32[]{:S(2)}) copy-start(bf16[4,4,128,128]{3,2,1,0:T(8,128)(2,1)} %get-tuple-element.189) | copy-start | bytes 1572868 | tf_op jit(solution)/shard_map/while
  264.1 3.5 %copy-start.2 = (bf16[4,4,768,128]{3,2,1,0:T(8,128)(2,1)S(1)}, bf16[4,4,768,128]{3,2,1,0:T(8,128)(2,1)}, u32[]{:S(2)}) copy-start(bf16[4,4,768,128]{3,2,1,0:T(8,128)(2,1)} %get-tuple-element.188) | copy-start | bytes 9437188 | tf_op jit(solution)/shard_map/while
  270.2 1.9 copy-start.3
  272.1 2.4 copy-start.4
Sparse Core Ops, SparseCore 0:
  12.1 173.6 all-gather.2
